TPU v7x, 256 devices: a whole 4x4x8 slice. The times are simulated.
256 devices in a mesh: col: 32 (over x, y, core), sub: 8 (over z).
Axes of the slice: x: 4, y: 4, z: 8, core: 2. Of those that a mesh axis runs over, the one named last changes fastest.
Arguments:
- vectors: bfloat16 [1048576, 128], P(('col', 'sub')), may hold values from -6 to 6
- near_blocks: bfloat16 [4096, 4, 256, 256], P(('col', 'sub')), may hold values from -0.1875 to 0.1875
- near_index: int32 [4096, 4], P(('col', 'sub')), may hold values from 0 to 4095, as said below
- leaf_basis: bfloat16 [4096, 32, 256], P(('col', 'sub')), may hold values from -0.375 to 0.375
- leaf_transfer: float32 [4096, 32, 32], P(('col', 'sub')), may hold values from -0.25 to 0.25
- leaf_coupling: float32 [4096, 8, 32, 32], P(('col', 'sub')), may hold values from -0.375 to 0.375
- leaf_far: int32 [4096, 8], P(('col', 'sub')), may hold values from 0 to 4095, as said below
- cluster_transfer: float32 [256, 32, 32], P(('col', 'sub')), may hold values from -0.375 to 0.375
- cluster_coupling: float32 [256, 4, 32, 32], P(('col', 'sub')), may hold values from -0.5 to 0.5
- cluster_partner: int32 [256, 4], P(('col', 'sub')), may hold values from 0 to 7
- top_coupling: float32 [32, 8, 32, 32], P('col'), may hold values from -0.375 to 0.375
- top_partner: int32 [32, 8], P('col'), may hold values from 0 to 31
Outputs:
- products: bfloat16 [1048576, 128], P(('col', 'sub'))
Inputs may be any that keep to these rules, and one draw needn't show every extreme that they name: `near_index`: slot 0 of leaf i is i itself; every entry lies within 16 leaves of i; slot 1 is exactly 16 leaves away from i. `leaf_far`: every entry lies within 16 leaves of its row leaf i; slots 0 and 1 are exactly 16 leaves away from i.
All inputs are finite; a program needn't handle non-finite values.
Results may differ from a plain program's by a relative error of at most 0.0034.
Values may be sent and summed in bfloat16 or wider, within the bound.
A program may use at most 64 MiB of HBM per device.

v0:
```python
import jax
import jax.numpy as jnp
from jax import lax
from jax.sharding import PartitionSpec as P

HIGHEST = lax.Precision.HIGHEST


def with_halo(block, sides, width):
    for axis, dim in sides:
        count = lax.axis_size(axis)
        forward = [(i, i + 1) for i in range(count - 1)]
        backward = [(target, source) for source, target in forward]
        low = lax.ppermute(
            lax.slice_in_dim(block, block.shape[dim] - width, None, axis=dim), axis, forward
        )
        high = lax.ppermute(lax.slice_in_dim(block, 0, width, axis=dim), axis, backward)
        block = jnp.concatenate([low, block, high], axis=dim)
    return block


def local(
    vectors,
    near_blocks,
    near_index,
    leaf_basis,
    leaf_transfer,
    leaf_coupling,
    leaf_far,
    cluster_transfer,
    cluster_coupling,
    cluster_partner,
    top_coupling,
    top_partner,
):
    leaves_here = leaf_basis.shape[0]
    leaf_rows = leaf_basis.shape[2]
    columns = vectors.shape[1]
    window_start = lax.axis_index(("col", "sub")) * leaves_here - leaves_here
    widened = with_halo(vectors, ((("col", "sub"), 0),), leaves_here * leaf_rows)
    window_vec = widened.reshape(3 * leaves_here, leaf_rows, columns)
    own_vec = vectors.reshape(leaves_here, leaf_rows, columns)
    leaf_coefs = jnp.einsum("lrp,lpc->lrc", leaf_basis, own_vec, preferred_element_type=jnp.float32)
    window_coefs = with_halo(leaf_coefs, ((("col", "sub"), 0),), leaves_here)
    cluster_coef = jnp.einsum("lrs,lrc->sc", leaf_transfer, leaf_coefs, precision=HIGHEST)
    sub_coefs = lax.all_gather(cluster_coef[None], "sub", axis=0, tiled=True)
    cluster_field = jnp.einsum(
        "krs,ksc->rc", cluster_coupling[0], sub_coefs[cluster_partner[0]], precision=HIGHEST
    )
    upward = jnp.dot(cluster_transfer[0].T, cluster_coef, precision=HIGHEST)
    top_coef = lax.psum(upward, "sub")
    col_coefs = lax.all_gather(top_coef[None], "col", axis=0, tiled=True)
    top_field = jnp.einsum(
        "krs,ksc->rc", top_coupling[0], col_coefs[top_partner[0]], precision=HIGHEST
    )
    cluster_field = cluster_field + jnp.dot(cluster_transfer[0], top_field, precision=HIGHEST)
    far_coefs = window_coefs[leaf_far - window_start]
    leaf_field = jnp.einsum("lkrs,lksc->lrc", leaf_coupling, far_coefs, precision=HIGHEST)
    leaf_field = leaf_field + jnp.einsum(
        "lrs,sc->lrc", leaf_transfer, cluster_field, precision=HIGHEST
    )
    rounded = leaf_field.astype(jnp.bfloat16)
    picked = window_vec[near_index - window_start]
    near_part = jnp.einsum(
        "lkij,lkjc->lic", near_blocks, picked, preferred_element_type=jnp.float32
    )
    far_part = jnp.einsum("lrp,lrc->lpc", leaf_basis, rounded, preferred_element_type=jnp.float32)
    return (near_part + far_part).astype(jnp.bfloat16).reshape(leaves_here * leaf_rows, columns)


def solution(mesh):
    in_specs = (
        P(("col", "sub"), None),
        P(("col", "sub"), None, None, None),
        P(("col", "sub"), None),
        P(("col", "sub"), None, None),
        P(("col", "sub"), None, None),
        P(("col", "sub"), None, None, None),
        P(("col", "sub"), None),
        P(("col", "sub"), None, None),
        P(("col", "sub"), None, None, None),
        P(("col", "sub"), None),
        P("col", None, None, None),
        P("col", None),
    )
    out_specs = P(("col", "sub"), None)
    return jax.shard_map(local, mesh=mesh, in_specs=in_specs, out_specs=out_specs, check_vma=False)
```

profile of v0, /device:TPU:1, one launch (start us, length us, event | category | flops | bytes accessed | tf_op | source)
XLA Modules:
  0.0 154.2 jit_solution(7868082268854348627)
XLA Ops:
  0.0 0.0 copy-start
  0.0 0.0 copy-start.5
  0.0 0.0 copy-start.4
  0.0 1.7 %fusion.12 = f32[16,32,128]{2,1,0:T(8,128)S(1)} fusion(bf16[16,32,256]{2,1,0:T(8,128)(2,1)} %param.15, bf16[16,256,128]{2,1,0:T(8,128)(2,1)} %bitcast.79), kind=kOutput, calls=%fused_computation.33 | convolution fusion | flops 33554432 | bytes 1572864 | tf_op jit(solution)/shard_map/lrp,lpc->lrc/dot_general | solution.py:43
  1.7 8.9 %collective-permute-start.3 = (f32[16,32,128]{2,1,0:T(8,128)S(1)}, f32[16,32,128]{2,1,0:T(8,128)S(1)}, u32[]{:S(2)}, u32[]{:S(2)}) collective-permute-start(f32[16,32,128]{2,1,0:T(8,128)S(1)} %fusion.12), channel_id=1, source_target_pairs={{1,0},{2,1},{3,2},{4,3},{5,4},{6,5},{7,6},{8,7},{9,8},{10,9},{11,1... | collective-permute-start | bytes 786440 | tf_op jit(solution)/shard_map/ppermute | solution.py:17
  10.6 1.9 %collective-permute-start.2 = (f32[16,32,128]{2,1,0:T(8,128)S(1)}, f32[16,32,128]{2,1,0:T(8,128)}, u32[]{:S(2)}, u32[]{:S(2)}) collective-permute-start(f32[16,32,128]{2,1,0:T(8,128)S(1)} %fusion.12), channel_id=1, source_target_pairs={{0,1},{1,2},{2,3},{3,4},{4,5},{5,6},{6,7},{7,8},{8,9},{9,10},{10,1... | collective-permute-start | bytes 786440 | tf_op jit(solution)/shard_map/ppermute | solution.py:14
  12.5 4.9 %collective-permute-start.1 = (bf16[4096,128]{1,0:T(8,128)(2,1)}, bf16[4096,128]{1,0:T(8,128)(2,1)}, u32[]{:S(2)}, u32[]{:S(2)}) collective-permute-start(bf16[4096,128]{1,0:T(8,128)(2,1)} %param.12), channel_id=1, source_target_pairs={{1,0},{2,1},{3,2},{4,3},{5,4},{6,5},{7,6},{8,7},{9,8},{10,9},{11,1... | collective-permute-start | bytes 3145736 | tf_op jit(solution)/shard_map/ppermute | solution.py:17
  17.4 1.9 %collective-permute-start = (bf16[4096,128]{1,0:T(8,128)(2,1)}, bf16[4096,128]{1,0:T(8,128)(2,1)}, u32[]{:S(2)}, u32[]{:S(2)}) collective-permute-start(bf16[4096,128]{1,0:T(8,128)(2,1)} %param.12), channel_id=1, source_target_pairs={{0,1},{1,2},{2,3},{3,4},{4,5},{5,6},{6,7},{7,8},{8,9},{9,10},{10,1... | collective-permute-start | bytes 3145736 | tf_op jit(solution)/shard_map/ppermute | solution.py:14
  19.3 0.7 fusion.10
  20.0 0.7 fusion.11
  20.7 1.3 compare_select_fusion.1
  21.9 0.7 compare_select_fusion
  22.6 0.6 pad_clamp_fusion
  23.2 0.1 copy.24
  23.3 0.6 reshape.78
  23.9 1.5 fusion.13
  25.4 0.9 convolution_bitcast_fusion.3
  26.4 35.0 %psum.7 = f32[1,32,128]{2,1,0:T(8,128)S(1)} all-reduce(f32[1,32,128]{2,1,0:T(8,128)S(1)} %convolution_bitcast_fusion.3), channel_id=1, replica_groups=mesh['col'=32,'sub'=8] {'sub'}, use_global_device_ids=true, to_apply=%region_0.0 | all-reduce | flops 4096 | bytes 32768 | tf_op jit(solution)/shard_map/psum | solution.py:51
  61.4 18.5 %all-gather = f32[256,128]{1,0:T(8,128)S(1)} all-gather(f32[32,128]{1,0:T(8,128)S(1)} %bitcast.81), channel_id=2, replica_groups=mesh['col'=32,'sub'=8] {'sub'}, dimensions={0}, use_global_device_ids=true | all-gather | bytes 147456 | tf_op jit(solution)/shard_map/all_gather | solution.py:46
  79.9 36.2 %all_gather.7 = f32[32,32,128]{2,1,0:T(8,128)S(1)} all-gather(f32[1,32,128]{2,1,0:T(8,128)S(1)} %psum.7), channel_id=1, replica_groups=mesh['col'=32,'sub'=8] {'col'}, dimensions={0}, use_global_device_ids=true | all-gather | bytes 540672 | tf_op jit(solution)/shard_map/all_gather | solution.py:52
  116.1 0.6 gather_fusion.2
  116.6 0.0 copy-done.5
  116.6 0.2 convolution_bitcast_fusion.4
  116.9 0.7 gather_fusion.3
  117.6 0.0 copy-done.4
  117.6 0.3 convolution_bitcast_fusion.2
  117.9 0.6 pad_clamp_fusion.2
  118.5 0.7 copy.22
  119.3 0.1 reshape.70
  119.4 0.9 fusion.4
  120.2 0.0 collective-permute-done.3
  120.3 0.0 collective-permute-done.2
  120.3 1.0 pad_maximum_fusion.1
  121.3 2.1 %gather_fusion.1 = f32[128,32,128]{2,1,0:T(8,128)} fusion(f32[48,32,128]{2,1,0:T(8,128)S(1)} %pad_maximum_fusion.1, s32[1024]{0:T(1024)S(1)} %pad_clamp_fusion.2), kind=kCustom, calls=%fused_computation.1 | custom fusion | bytes 4194816 | tf_op jit(solution)/shard_map/gather | solution.py:57
  123.4 0.0 copy-start.3
  123.4 0.0 copy-done
  123.4 4.4 %convolution_bitcast_fusion.1 = f32[16,32,128]{2,1,0:T(8,128)S(1)} fusion(f32[16,8,32,128]{3,2,1,0:T(8,128)} %bitcast.78, f32[16,8,32,32]{3,2,1,0:T(8,128)S(1)} %copy-done), kind=kOutput, calls=%fused_computation.10 | convolution fusion | flops 201326592 | bytes 2883584 | tf_op jit(solution)/shard_map/lkrs,lksc->lrc/dot_general | solution.py:58
  127.9 0.0 copy-done.3
  127.9 0.4 fusion.3
  128.2 0.0 copy-done.2
  128.2 1.9 %fusion.14 = f32[16,128,256]{2,1,0:T(8,128)} fusion(bf16[16,32,128]{2,1,0:T(8,128)(2,1)S(1)} %fusion.3, bf16[16,32,256]{2,1,0:T(8,128)(2,1)S(1)} %copy-done.2), kind=kOutput, calls=%fused_computation.35 | convolution fusion | flops 33554432 | bytes 2490368 | tf_op jit(solution)/shard_map/lrp,lrc->lpc/dot_general | solution.py:67
  130.1 0.0 collective-permute-done.1
  130.1 0.0 collective-permute-done
  130.1 0.0 copy-done.1
  130.1 9.8 %pad_maximum_fusion = bf16[12288,128]{1,0:T(8,128)(2,1)} fusion(bf16[4096,128]{1,0:T(8,128)(2,1)} %collective-permute-done.1, bf16[4096,128]{1,0:T(8,128)(2,1)S(1)} %copy-done.1, bf16[4096,128]{1,0:T(8,128)(2,1)} %collective-permute-done), kind=kLoop, calls=%fused_computation.4 | loop fusion | flops 9437184 | bytes 6291456 | tf_op jit(solution)/shard_map/concatenate | solution.py:18
  139.9 4.9 %gather_fusion = bf16[64,256,128]{2,1,0:T(8,128)(2,1)} fusion(bf16[48,256,128]{2,1,0:T(8,128)(2,1)} %bitcast.76, s32[1024]{0:T(1024)S(1)} %pad_clamp_fusion.3), kind=kCustom, calls=%fused_computation | custom fusion | bytes 8388864 | tf_op jit(solution)/shard_map/gather | solution.py:63
  144.8 8.1 %fusion.1 = bf16[16,256,128]{1,2,0:T(8,128)(2,1)S(1)} fusion(f32[16,128,256]{2,1,0:T(8,128)} %fusion.14, bf16[16,4,256,128]{3,2,1,0:T(8,128)(2,1)} %bitcast.77, bf16[16,4,256,256]{3,2,1,0:T(8,128)(2,1)} %param.13), kind=kOutput, calls=%fused_computation.7 | convolution fusion | flops 1074790400 | bytes 15728640 | tf_op jit(solution)/shard_map/lkij,lkjc->lic/dot_general | solution.py:64
  152.9 1.3 copy.26
  (4 shorter events, 0.0 us)
Async XLA Ops:
  0.0 123.4 %copy-start = (f32[16,8,32,32]{3,2,1,0:T(8,128)S(1)}, f32[16,8,32,32]{3,2,1,0:T(8,128)}, u32[]{:S(2)}) copy-start(f32[16,8,32,32]{3,2,1,0:T(8,128)} %param.17) | copy-start | bytes 1572868
  0.0 116.6 %copy-start.5 = (f32[1,4,32,32]{3,2,1,0:T(8,128)S(1)}, f32[1,4,32,32]{3,2,1,0:T(8,128)}, u32[]{:S(2)}) copy-start(f32[1,4,32,32]{3,2,1,0:T(8,128)} %param.20) | copy-start | bytes 49156
  0.0 117.6 %copy-start.4 = (f32[1,8,32,32]{3,2,1,0:T(8,128)S(1)}, f32[1,8,32,32]{3,2,1,0:T(8,128)}, u32[]{:S(2)}) copy-start(f32[1,8,32,32]{3,2,1,0:T(8,128)} %param.22) | copy-start | bytes 98308
  1.7 118.5 %collective-permute-start.3 = (f32[16,32,128]{2,1,0:T(8,128)S(1)}, f32[16,32,128]{2,1,0:T(8,128)S(1)}, u32[]{:S(2)}, u32[]{:S(2)}) collective-permute-start(f32[16,32,128]{2,1,0:T(8,128)S(1)} %fusion.12), channel_id=1, source_target_pairs={{1,0},{2,1},{3,2},{4,3},{5,4},{6,5},{7,6},{8,7},{9,8},{10,9},{11,1... | collective-permute-start | bytes 786440 | tf_op jit(solution)/shard_map/ppermute | solution.py:17
  10.6 109.6 %collective-permute-start.2 = (f32[16,32,128]{2,1,0:T(8,128)S(1)}, f32[16,32,128]{2,1,0:T(8,128)}, u32[]{:S(2)}, u32[]{:S(2)}) collective-permute-start(f32[16,32,128]{2,1,0:T(8,128)S(1)} %fusion.12), channel_id=1, source_target_pairs={{0,1},{1,2},{2,3},{3,4},{4,5},{5,6},{6,7},{7,8},{8,9},{9,10},{10,1... | collective-permute-start | bytes 786440 | tf_op jit(solution)/shard_map/ppermute | solution.py:14
  12.5 117.6 %collective-permute-start.1 = (bf16[4096,128]{1,0:T(8,128)(2,1)}, bf16[4096,128]{1,0:T(8,128)(2,1)}, u32[]{:S(2)}, u32[]{:S(2)}) collective-permute-start(bf16[4096,128]{1,0:T(8,128)(2,1)} %param.12), channel_id=1, source_target_pairs={{1,0},{2,1},{3,2},{4,3},{5,4},{6,5},{7,6},{8,7},{9,8},{10,9},{11,1... | collective-permute-start | bytes 3145736 | tf_op jit(solution)/shard_map/ppermute | solution.py:17
  17.4 112.7 %collective-permute-start = (bf16[4096,128]{1,0:T(8,128)(2,1)}, bf16[4096,128]{1,0:T(8,128)(2,1)}, u32[]{:S(2)}, u32[]{:S(2)}) collective-permute-start(bf16[4096,128]{1,0:T(8,128)(2,1)} %param.12), channel_id=1, source_target_pairs={{0,1},{1,2},{2,3},{3,4},{4,5},{5,6},{6,7},{7,8},{8,9},{9,10},{10,1... | collective-permute-start | bytes 3145736 | tf_op jit(solution)/shard_map/ppermute | solution.py:14
  123.4 4.4 %copy-start.3 = (f32[16,32,32]{2,1,0:T(8,128)S(1)}, f32[16,32,32]{2,1,0:T(8,128)}, u32[]{:S(2)}) copy-start(f32[16,32,32]{2,1,0:T(8,128)} %param.16) | copy-start | bytes 196612
  123.4 4.8 %copy-start.2 = (bf16[16,32,256]{2,1,0:T(8,128)(2,1)S(1)}, bf16[16,32,256]{2,1,0:T(8,128)(2,1)}, u32[]{:S(2)}) copy-start(bf16[16,32,256]{2,1,0:T(8,128)(2,1)} %param.15) | copy-start | bytes 786436
  123.4 6.7 %copy-start.1 = (bf16[4096,128]{1,0:T(8,128)(2,1)S(1)}, bf16[4096,128]{1,0:T(8,128)(2,1)}, u32[]{:S(2)}) copy-start(bf16[4096,128]{1,0:T(8,128)(2,1)} %param.12) | copy-start | bytes 3145732
where the time goes:
time: 155 us; the launch traced here: 154 us
  blocking collectives  89.7 us (58%)
  matrix products  20.3 us (13%)
  starting transfers between devices  17.6 us (11%)
  other arithmetic  15.3 us (10%)
  local copies, waits for them, and re-layouts  11.1 us (7%)
    all_gather x1, blocking collectives, local(): col_coefs = lax.all_gather(top_coef[None], 'col', axis=0, tiled=True)  36.2 us
    psum x1, blocking collectives, local(): top_coef = lax.psum(upward, 'sub')  35 us
    all_gather x1, blocking collectives, local(): sub_coefs = lax.all_gather(cluster_coef[None], 'sub', axis=0, tiled=True)  18.5 us
    ppermute x2, starting transfers between devices, with_halo(): lax.ppermute(lax.slice_in_dim(block, 0, width, axis=dim), axis, backward)  13.7 us
    concatenate x2, other arithmetic, with_halo(): block = jnp.concatenate([low, block, high], axis=dim)  10.8 us
    dot_general x1, matrix products, local(): jnp.einsum('lkij,lkjc->lic', near_blocks, picked, preferred_element_type=...  8.06 us
    gather x1, local copies, waits for them, and re-layouts, local(): picked = window_vec[near_index - window_start]  4.91 us
    dot_general x1, matrix products, local(): jnp.einsum('lkrs,lksc->lrc', leaf_coupling, far_coefs, precision=HIGHEST)  4.43 us
  transfers between devices with their start and end apart: 4, of which 0 were waited for; matrix products, arithmetic and copies ran while one was open for 14% of the time, Pallas kernels for 0%

commit v1 on v0

--- a/solution.py
+++ b/solution.py
@@ -48,7 +48,7 @@
         "krs,ksc->rc", cluster_coupling[0], sub_coefs[cluster_partner[0]], precision=HIGHEST
     )
     upward = jnp.dot(cluster_transfer[0].T, cluster_coef, precision=HIGHEST)
-    top_coef = lax.psum(upward, "sub")
+    top_coef = jnp.sum(lax.all_gather(upward, "sub"), axis=0)
     col_coefs = lax.all_gather(top_coef[None], "col", axis=0, tiled=True)
     top_field = jnp.einsum(
         "krs,ksc->rc", top_coupling[0], col_coefs[top_partner[0]], precision=HIGHEST

time: 155 us -> 155 us (level)
    psum x1 -> x0, blocking collectives: 35 us -> none  [local(): top_coef = lax.psum(upward, 'sub')]
    all_gather x0 -> x1, blocking collectives: none -> 34.2 us  [local(): top_coef = jnp.sum(lax.all_gather(upward, 'sub'), axis=0)]
where the time goes in v1:
time: 155 us; the launch traced here: 154 us
  blocking collectives  88.2 us (57%)
  matrix products  21.6 us (14%)
  starting transfers between devices  17.6 us (11%)
  other arithmetic  15.3 us (10%)
  local copies, waits for them, and re-layouts  11.1 us (7%)
    all_gather x1, blocking collectives, local(): col_coefs = lax.all_gather(top_coef[None], 'col', axis=0, tiled=True)  35.8 us
    all_gather x1, blocking collectives, local(): top_coef = jnp.sum(lax.all_gather(upward, 'sub'), axis=0)  34.2 us
    all_gather x1, blocking collectives, local(): sub_coefs = lax.all_gather(cluster_coef[None], 'sub', axis=0, tiled=True)  18.2 us
    ppermute x2, starting transfers between devices, with_halo(): lax.ppermute(lax.slice_in_dim(block, 0, width, axis=dim), axis, backward)  13.7 us
    concatenate x2, other arithmetic, with_halo(): block = jnp.concatenate([low, block, high], axis=dim)  10.8 us
    dot_general x1, matrix products, local(): jnp.einsum('lkij,lkjc->lic', near_blocks, picked, preferred_element_type=...  8.07 us
    gather x1, local copies, waits for them, and re-layouts, local(): picked = window_vec[near_index - window_start]  4.91 us
    dot_general x1, matrix products, local(): jnp.einsum('lkrs,lksc->lrc', leaf_coupling, far_coefs, precision=HIGHEST)  4.43 us
  transfers between devices with their start and end apart: 4, of which 0 were waited for; matrix products, arithmetic and copies ran while one was open for 14% of the time, Pallas kernels for 0%

profile of v1, /device:TPU:1, one launch (start us, length us, event | category | flops | bytes accessed | tf_op | source)
XLA Modules:
  0.0 154.0 jit_solution(15179911178422718816)
XLA Ops:
  0.0 0.0 copy-start
  0.0 0.0 copy-start.5
  0.0 0.0 copy-start.4
  0.0 1.7 %fusion.12 = f32[16,32,128]{2,1,0:T(8,128)S(1)} fusion(bf16[16,32,256]{2,1,0:T(8,128)(2,1)} %param.15, bf16[16,256,128]{2,1,0:T(8,128)(2,1)} %bitcast.79), kind=kOutput, calls=%fused_computation.33 | convolution fusion | flops 33554432 | bytes 1572864 | tf_op jit(solution)/shard_map/lrp,lpc->lrc/dot_general | solution.py:43
  1.8 8.9 %collective-permute-start.3 = (f32[16,32,128]{2,1,0:T(8,128)S(1)}, f32[16,32,128]{2,1,0:T(8,128)S(1)}, u32[]{:S(2)}, u32[]{:S(2)}) collective-permute-start(f32[16,32,128]{2,1,0:T(8,128)S(1)} %fusion.12), channel_id=1, source_target_pairs={{1,0},{2,1},{3,2},{4,3},{5,4},{6,5},{7,6},{8,7},{9,8},{10,9},{11,1... | collective-permute-start | bytes 786440 | tf_op jit(solution)/shard_map/ppermute | solution.py:17
  10.6 1.9 %collective-permute-start.2 = (f32[16,32,128]{2,1,0:T(8,128)S(1)}, f32[16,32,128]{2,1,0:T(8,128)}, u32[]{:S(2)}, u32[]{:S(2)}) collective-permute-start(f32[16,32,128]{2,1,0:T(8,128)S(1)} %fusion.12), channel_id=1, source_target_pairs={{0,1},{1,2},{2,3},{3,4},{4,5},{5,6},{6,7},{7,8},{8,9},{9,10},{10,1... | collective-permute-start | bytes 786440 | tf_op jit(solution)/shard_map/ppermute | solution.py:14
  12.6 4.9 %collective-permute-start.1 = (bf16[4096,128]{1,0:T(8,128)(2,1)}, bf16[4096,128]{1,0:T(8,128)(2,1)}, u32[]{:S(2)}, u32[]{:S(2)}) collective-permute-start(bf16[4096,128]{1,0:T(8,128)(2,1)} %param.12), channel_id=1, source_target_pairs={{1,0},{2,1},{3,2},{4,3},{5,4},{6,5},{7,6},{8,7},{9,8},{10,9},{11,1... | collective-permute-start | bytes 3145736 | tf_op jit(solution)/shard_map/ppermute | solution.py:17
  17.4 1.9 %collective-permute-start = (bf16[4096,128]{1,0:T(8,128)(2,1)}, bf16[4096,128]{1,0:T(8,128)(2,1)}, u32[]{:S(2)}, u32[]{:S(2)}) collective-permute-start(bf16[4096,128]{1,0:T(8,128)(2,1)} %param.12), channel_id=1, source_target_pairs={{0,1},{1,2},{2,3},{3,4},{4,5},{5,6},{6,7},{7,8},{8,9},{9,10},{10,1... | collective-permute-start | bytes 3145736 | tf_op jit(solution)/shard_map/ppermute | solution.py:14
  19.4 0.7 fusion.10
  20.0 0.7 fusion.11
  20.7 1.3 compare_select_fusion.1
  22.0 0.7 compare_select_fusion
  22.6 0.6 pad_clamp_fusion
  23.3 0.1 copy.19
  23.3 0.6 reshape.78
  23.9 1.5 fusion.13
  25.4 0.9 convolution_bitcast_fusion.4
  26.4 34.2 %all-gather.1 = f32[256,128]{1,0:T(8,128)S(1)} all-gather(f32[32,128]{1,0:T(8,128)S(1)} %convolution_bitcast_fusion.4), channel_id=3, replica_groups=mesh['col'=32,'sub'=8] {'sub'}, dimensions={0}, use_global_device_ids=true | all-gather | bytes 147456 | tf_op jit(solution)/shard_map/all_gather | solution.py:51
  60.6 18.2 %all-gather = f32[256,128]{1,0:T(8,128)S(1)} all-gather(f32[32,128]{1,0:T(8,128)S(1)} %bitcast.83), channel_id=2, replica_groups=mesh['col'=32,'sub'=8] {'sub'}, dimensions={0}, use_global_device_ids=true | all-gather | bytes 147456 | tf_op jit(solution)/shard_map/all_gather | solution.py:46
  78.8 35.8 %all-gather.2 = f32[1024,128]{1,0:T(8,128)S(1)} all-gather(f32[32,128]{1,0:T(8,128)S(1)} %reduce_sum.9), channel_id=4, replica_groups=mesh['col'=32,'sub'=8] {'col'}, dimensions={0}, use_global_device_ids=true | all-gather | bytes 540672 | tf_op jit(solution)/shard_map/all_gather | solution.py:52
  114.6 0.6 gather_fusion.2
  115.2 1.4 convolution_bitcast_fusion.3
  116.6 0.7 gather_fusion.3
  117.3 0.0 copy-done.4
  117.3 1.0 convolution_bitcast_fusion.2
  118.3 0.6 pad_clamp_fusion.2
  119.0 0.7 copy.17
  119.7 0.1 reshape.70
  119.8 0.0 copy-done.5
  119.8 0.2 fusion.4
  120.0 0.0 collective-permute-done.3
  120.0 0.0 collective-permute-done.2
  120.0 1.0 pad_maximum_fusion.1
  121.0 2.1 %gather_fusion.1 = f32[128,32,128]{2,1,0:T(8,128)} fusion(f32[48,32,128]{2,1,0:T(8,128)S(1)} %pad_maximum_fusion.1, s32[1024]{0:T(1024)S(1)} %pad_clamp_fusion.2), kind=kCustom, calls=%fused_computation.1 | custom fusion | bytes 4194816 | tf_op jit(solution)/shard_map/gather | solution.py:57
  123.2 0.0 copy-start.3
  123.2 0.0 copy-done
  123.2 4.4 %convolution_bitcast_fusion.1 = f32[16,32,128]{2,1,0:T(8,128)S(1)} fusion(f32[16,8,32,128]{3,2,1,0:T(8,128)} %bitcast.78, f32[16,8,32,32]{3,2,1,0:T(8,128)S(1)} %copy-done), kind=kOutput, calls=%fused_computation.10 | convolution fusion | flops 201326592 | bytes 2883584 | tf_op jit(solution)/shard_map/lkrs,lksc->lrc/dot_general | solution.py:58
  127.6 0.0 copy-done.3
  127.6 0.4 fusion.3
  128.0 0.0 copy-done.2
  128.0 1.9 %fusion.14 = f32[16,128,256]{2,1,0:T(8,128)} fusion(bf16[16,32,128]{2,1,0:T(8,128)(2,1)S(1)} %fusion.3, bf16[16,32,256]{2,1,0:T(8,128)(2,1)S(1)} %copy-done.2), kind=kOutput, calls=%fused_computation.35 | convolution fusion | flops 33554432 | bytes 2490368 | tf_op jit(solution)/shard_map/lrp,lrc->lpc/dot_general | solution.py:67
  129.9 0.0 collective-permute-done.1
  129.9 0.0 collective-permute-done
  129.9 0.0 copy-done.1
  129.9 9.8 %pad_maximum_fusion = bf16[12288,128]{1,0:T(8,128)(2,1)} fusion(bf16[4096,128]{1,0:T(8,128)(2,1)} %collective-permute-done.1, bf16[4096,128]{1,0:T(8,128)(2,1)S(1)} %copy-done.1, bf16[4096,128]{1,0:T(8,128)(2,1)} %collective-permute-done), kind=kLoop, calls=%fused_computation.4 | loop fusion | flops 9437184 | bytes 6291456 | tf_op jit(solution)/shard_map/concatenate | solution.py:18
  139.7 4.9 %gather_fusion = bf16[64,256,128]{2,1,0:T(8,128)(2,1)} fusion(bf16[48,256,128]{2,1,0:T(8,128)(2,1)} %bitcast.76, s32[1024]{0:T(1024)S(1)} %pad_clamp_fusion.3), kind=kCustom, calls=%fused_computation | custom fusion | bytes 8388864 | tf_op jit(solution)/shard_map/gather | solution.py:63
  144.6 8.1 %fusion.1 = bf16[16,256,128]{1,2,0:T(8,128)(2,1)S(1)} fusion(f32[16,128,256]{2,1,0:T(8,128)} %fusion.14, bf16[16,4,256,128]{3,2,1,0:T(8,128)(2,1)} %bitcast.77, bf16[16,4,256,256]{3,2,1,0:T(8,128)(2,1)} %param.13), kind=kOutput, calls=%fused_computation.7 | convolution fusion | flops 1074790400 | bytes 15728640 | tf_op jit(solution)/shard_map/lkij,lkjc->lic/dot_general | solution.py:64
  152.7 1.3 copy.21
  (5 shorter events, 0.0 us)
Async XLA Ops:
  0.0 123.2 %copy-start = (f32[16,8,32,32]{3,2,1,0:T(8,128)S(1)}, f32[16,8,32,32]{3,2,1,0:T(8,128)}, u32[]{:S(2)}) copy-start(f32[16,8,32,32]{3,2,1,0:T(8,128)} %param.17) | copy-start | bytes 1572868
  0.0 119.8 %copy-start.5 = (f32[1,32,32]{2,1,0:T(8,128)S(1)}, f32[1,32,32]{2,1,0:T(8,128)}, u32[]{:S(2)}) copy-start(f32[1,32,32]{2,1,0:T(8,128)} %param.19) | copy-start | bytes 12292
  0.0 117.3 %copy-start.4 = (f32[1,8,32,32]{3,2,1,0:T(8,128)S(1)}, f32[1,8,32,32]{3,2,1,0:T(8,128)}, u32[]{:S(2)}) copy-start(f32[1,8,32,32]{3,2,1,0:T(8,128)} %param.22) | copy-start | bytes 98308
  1.8 118.3 %collective-permute-start.3 = (f32[16,32,128]{2,1,0:T(8,128)S(1)}, f32[16,32,128]{2,1,0:T(8,128)S(1)}, u32[]{:S(2)}, u32[]{:S(2)}) collective-permute-start(f32[16,32,128]{2,1,0:T(8,128)S(1)} %fusion.12), channel_id=1, source_target_pairs={{1,0},{2,1},{3,2},{4,3},{5,4},{6,5},{7,6},{8,7},{9,8},{10,9},{11,1... | collective-permute-start | bytes 786440 | tf_op jit(solution)/shard_map/ppermute | solution.py:17
  10.6 109.4 %collective-permute-start.2 = (f32[16,32,128]{2,1,0:T(8,128)S(1)}, f32[16,32,128]{2,1,0:T(8,128)}, u32[]{:S(2)}, u32[]{:S(2)}) collective-permute-start(f32[16,32,128]{2,1,0:T(8,128)S(1)} %fusion.12), channel_id=1, source_target_pairs={{0,1},{1,2},{2,3},{3,4},{4,5},{5,6},{6,7},{7,8},{8,9},{9,10},{10,1... | collective-permute-start | bytes 786440 | tf_op jit(solution)/shard_map/ppermute | solution.py:14
  12.6 117.3 %collective-permute-start.1 = (bf16[4096,128]{1,0:T(8,128)(2,1)}, bf16[4096,128]{1,0:T(8,128)(2,1)}, u32[]{:S(2)}, u32[]{:S(2)}) collective-permute-start(bf16[4096,128]{1,0:T(8,128)(2,1)} %param.12), channel_id=1, source_target_pairs={{1,0},{2,1},{3,2},{4,3},{5,4},{6,5},{7,6},{8,7},{9,8},{10,9},{11,1... | collective-permute-start | bytes 3145736 | tf_op jit(solution)/shard_map/ppermute | solution.py:17
  17.4 112.5 %collective-permute-start = (bf16[4096,128]{1,0:T(8,128)(2,1)}, bf16[4096,128]{1,0:T(8,128)(2,1)}, u32[]{:S(2)}, u32[]{:S(2)}) collective-permute-start(bf16[4096,128]{1,0:T(8,128)(2,1)} %param.12), channel_id=1, source_target_pairs={{0,1},{1,2},{2,3},{3,4},{4,5},{5,6},{6,7},{7,8},{8,9},{9,10},{10,1... | collective-permute-start | bytes 3145736 | tf_op jit(solution)/shard_map/ppermute | solution.py:14
  123.2 4.4 %copy-start.3 = (f32[16,32,32]{2,1,0:T(8,128)S(1)}, f32[16,32,32]{2,1,0:T(8,128)}, u32[]{:S(2)}) copy-start(f32[16,32,32]{2,1,0:T(8,128)} %param.16) | copy-start | bytes 196612
  123.2 4.9 %copy-start.2 = (bf16[16,32,256]{2,1,0:T(8,128)(2,1)S(1)}, bf16[16,32,256]{2,1,0:T(8,128)(2,1)}, u32[]{:S(2)}) copy-start(bf16[16,32,256]{2,1,0:T(8,128)(2,1)} %param.15) | copy-start | bytes 786436
  123.2 6.7 %copy-start.1 = (bf16[4096,128]{1,0:T(8,128)(2,1)S(1)}, bf16[4096,128]{1,0:T(8,128)(2,1)}, u32[]{:S(2)}) copy-start(bf16[4096,128]{1,0:T(8,128)(2,1)} %param.12) | copy-start | bytes 3145732
